TPU v7x, 256 devices: a whole 4x4x8 slice. The times are simulated.
256 devices in a mesh: section: 32 (over y, x, z_lo), dp: 8 (over z_hi, core).
Axes of the slice: x: 4, y: 4, z: 8 (z_hi: 4, z_lo: 2; z = z_hi * 2 + z_lo), core: 2. Of those that a mesh axis runs over, the one named last changes fastest.
Arguments:
- act_down: bfloat16 [32, 2, 2048, 1024], P('section', None, 'dp'), may hold values from -6 to 6
- act_up: bfloat16 [32, 2, 2048, 1024], P('section', None, 'dp'), may hold values from -6 to 6
- grad_down: bfloat16 [32, 2048, 1024], P('section', 'dp'), may hold values from -1.5 to 1.5
- grad_up: bfloat16 [32, 2048, 1024], P('section', 'dp'), may hold values from -1.5 to 1.5
- seed_down: bfloat16 [2048, 1024], P('dp'), may hold values from -1.5 to 1.5
- seed_up: bfloat16 [2048, 1024], P('dp'), may hold values from -1.5 to 1.5
- gain_down: float32 [32, 1024], P('section'), as said below
- qkv_down: bfloat16 [32, 1024, 768], P('section'), as said below
- outproj_down: bfloat16 [32, 512, 1024], P('section'), as said below
- gain_up: float32 [32, 1024], P('section'), as said below
- qkv_up: bfloat16 [32, 1024, 768], P('section'), as said below
- outproj_up: bfloat16 [32, 512, 1024], P('section'), as said below
- doc_offsets: int32 [2, 32, 2, 8], P(None, 'section', None, 'dp'), may hold values from 1 to 255
- slot_order: int32 [2, 32, 2], P(None, 'section'), may hold values from 0 to 1, each once within a row
Outputs:
- input_grads: bfloat16 [2, 32, 2, 2048, 1024], P(None, 'section', None, 'dp')
- grad_gain: float32 [32, 1024], P('section', 'dp')
- grad_qkv: float32 [32, 1024, 768], P('section', 'dp')
- grad_outproj: float32 [32, 512, 1024], P('section', 'dp')
Inputs may be any that keep to these rules, and one draw needn't show every extreme that they name: `gain_down`: the down copy of every layer. `qkv_down`: the down copy of every layer. `outproj_down`: the down copy of every layer. gain_up[s] equals gain_down[31 - s]. qkv_up[s] equals qkv_down[31 - s]. outproj_up[s] equals outproj_down[31 - s]. `doc_offsets`: each sequence holds two documents; the value is the position where the second begins. `slot_order`: each row of a direction and section names 0 and 1 once each.
All inputs are finite; a program needn't handle non-finite values.
Results may differ from a plain program's by a relative error of at most 0.015.
Values may be sent and summed in bfloat16 or wider, within the bound.
A program may use at most 128 MiB of HBM per device.

v0:
```python
import jax
import jax.numpy as jnp
from jax import lax
from jax.experimental import pallas as pl
from jax.experimental.pallas import tpu as pltpu
from jax.sharding import PartitionSpec as P

F32, BF16 = jnp.float32, jnp.bfloat16
EPSILON = 1e-05
D, SEQ, HEADS, GROUP, HD = 1024, 256, 8, 4, 64
QW, QKV = 512, 768
ROWS = 32
PIECE = QKV + QW + 16


def nn(a, b):
    return jnp.dot(a, b, preferred_element_type=F32)


def nt(a, b):
    return lax.dot_general(a, b, (((1,), (1,)), ((), ())), preferred_element_type=F32)


def norm_rows(x, gain, normed, inverse):
    @pl.loop(0, SEQ // ROWS)
    def _(step):
        rows = pl.ds(pl.multiple_of(step * ROWS, ROWS), ROWS)
        xf = x[rows, :].astype(F32)
        inv = lax.rsqrt(jnp.mean(xf * xf, axis=1, keepdims=True) + EPSILON)
        normed[rows, :] = (xf * inv * gain[...]).astype(BF16)
        inverse[rows, :] = jnp.broadcast_to(inv, (ROWS, 128))


def forward(offset, normed, qkv, keep):
    proj_t, keys, values, soft, soft_low, att_t = keep
    for n in range(3):
        cols = slice(n * 256, n * 256 + 256)
        part = nn(normed[...], qkv[:, cols])
        proj_t[cols, :] = part.T.astype(BF16)
        if n == 2:
            low = part.astype(BF16)
            keys[0], keys[1] = low[:, :64], low[:, 64:128]
            values[0], values[1] = low[:, 128:192], low[:, 192:256]

    @pl.loop(0, HEADS)
    def _(head):
        group = head // GROUP
        rows = pl.ds(pl.multiple_of(head * HD, HD), HD)
        scores = nn(keys[group], proj_t[rows, :])
        for half, depth in ((0, 128), (1, 256)):
            cols = slice(half * 128, half * 128 + 128)
            at_key = lax.broadcasted_iota(jnp.int32, (depth, 128), 0)
            at_query = lax.broadcasted_iota(jnp.int32, (depth, 128), 1) + half * 128
            allowed = (at_key <= at_query) & ((at_query < offset) | (at_key >= offset))
            part = jnp.where(allowed, scores[:depth, cols] * (HD**-0.5), -1e30)
            raised = jnp.exp(part - jnp.max(part, axis=0, keepdims=True))
            weights = raised * (1.0 / jnp.sum(raised, axis=0, keepdims=True))
            soft[head, :depth, cols] = weights
            soft_low[head, :depth, cols] = weights.astype(BF16)
        soft_low[head, 128:, :128] = jnp.zeros((128, 128), BF16)
        value_rows = pl.ds(pl.multiple_of(QW + 128 + group * HD, HD), HD)
        att_t[rows, :] = nn(proj_t[value_rows, :], soft_low[head]).astype(BF16)


def backward(x, gain, inverse, qkv, outproj, upstream, keep, work, grad_t, gain_sum, result):
    proj_t, keys, values, soft, soft_low, att_t = keep
    att_grad, score_grad, key_sum, value_sum, grad, normed_grad = work
    for m in range(2):
        rows = slice(m * 256, m * 256 + 256)
        att_grad[rows, :] = nt(outproj[rows, :], upstream[...]).astype(BF16)
    key_sum[...] = jnp.zeros_like(key_sum)
    value_sum[...] = jnp.zeros_like(value_sum)
    score_grad[128:, :128] = jnp.zeros((128, 128), BF16)

    @pl.loop(0, HEADS)
    def _(head):
        group = head // GROUP
        rows = pl.ds(pl.multiple_of(head * HD, HD), HD)
        low = att_grad[rows, :]
        soft_grad = nn(values[group], low)
        for half, depth in ((0, 128), (1, 256)):
            cols = slice(half * 128, half * 128 + 128)
            weights = soft[head, :depth, cols]
            part = soft_grad[:depth, cols]
            total = jnp.sum(weights * part, axis=0, keepdims=True)
            score_grad[:depth, cols] = (weights * (part - total) * (HD**-0.5)).astype(BF16)
        key_rows = pl.ds(pl.multiple_of(QW + group * HD, HD), HD)
        grad_t[rows, :] = nn(proj_t[key_rows, :], score_grad[...]).astype(BF16)
        key_sum[group] += nt(proj_t[rows, :], score_grad[...])
        value_sum[group] += nt(low, soft_low[head])

    for g in range(2):
        grad_t[QW + g * HD : QW + g * HD + HD, :] = key_sum[g].astype(BF16)
        grad_t[QW + 128 + g * HD : QW + 128 + g * HD + HD, :] = value_sum[g].astype(BF16)
    for n in range(3):
        cols = slice(n * 256, n * 256 + 256)
        grad[:, cols] = grad_t[cols, :].T
    for n in range(4):
        cols = slice(n * 256, n * 256 + 256)
        normed_grad[:, cols] = nt(grad[...], qkv[cols, :])

    @pl.loop(0, SEQ // ROWS)
    def _(step):
        rows = pl.ds(pl.multiple_of(step * ROWS, ROWS), ROWS)
        inv = inverse[rows, :][:, :1]
        scaled = x[rows, :].astype(F32) * inv
        hat = normed_grad[rows, :]
        both = hat * scaled
        partial = both[:8]
        for k in range(1, ROWS // 8):
            partial = partial + both[k * 8 : k * 8 + 8]
        gain_sum[...] += partial
        mean = jnp.mean(both * gain[...], axis=1, keepdims=True)
        moved = inv * (hat * gain[...] - scaled * mean)
        result[rows, :] = (upstream[rows, :].astype(F32) + moved).astype(BF16)


def weight_terms(q, grad_t, normed, att_t, upstream, gain_sum, piece):
    cols = pl.ds(pl.multiple_of(q * 256, 256), 256)
    for m in range(3):
        rows = slice(m * 256, m * 256 + 256)
        part = nn(grad_t[0][rows, :], normed[0][:, cols]) + nn(grad_t[1][rows, :], normed[1][:, cols])
        for core in range(2):
            piece[core, rows, :] = part[:, core * 128 : core * 128 + 128].astype(BF16)
    heads = pl.ds(pl.multiple_of(q * 128, 128), 128)
    for n in range(4):
        wide = slice(n * 256, n * 256 + 256)
        part = nn(att_t[0][heads, :], upstream[0][:, wide]) + nn(att_t[1][heads, :], upstream[1][:, wide])
        for core in range(2):
            for k in range(2):
                at = QKV + (2 * n + k) * HD
                block = part[core * HD : core * HD + HD, k * 128 : k * 128 + 128]
                piece[core, at : at + HD, :] = block.astype(BF16)
    for core in range(2):
        lanes = pl.ds(pl.multiple_of(q * 256 + core * 128, 128), 128)
        row = jnp.sum(gain_sum[:, lanes], axis=0, keepdims=True)
        piece[core, QKV + QW :, :] = jnp.broadcast_to(row, (16, 128)).astype(BF16)


KEEP = [
    pltpu.VMEM((QKV, SEQ), BF16),
    pltpu.VMEM((2, SEQ, HD), BF16),
    pltpu.VMEM((2, SEQ, HD), BF16),
    pltpu.VMEM((HEADS, SEQ, SEQ), F32),
    pltpu.VMEM((HEADS, SEQ, SEQ), BF16),
]
WORK = [
    pltpu.VMEM((QW, SEQ), BF16),
    pltpu.VMEM((SEQ, SEQ), BF16),
    pltpu.VMEM((2, HD, SEQ), F32),
    pltpu.VMEM((2, HD, SEQ), F32),
    pltpu.VMEM((SEQ, QKV), BF16),
    pltpu.VMEM((SEQ, D), F32),
]
INV = pltpu.VMEM((SEQ, 128), F32)


def first_kernel(picks, x, gain, qkv, outproj, upstream, result, normed, grad_t, att_t, gain_sum, inverse, *scratch):
    keep, work = (*scratch[:5], att_t), scratch[5:]
    gain_sum[...] = jnp.zeros_like(gain_sum)
    norm_rows(x, gain, normed, inverse)
    forward(picks[1], normed, qkv, keep)
    backward(x, gain, inverse, qkv, outproj, upstream, keep, work, grad_t, gain_sum, result)


def second_kernel(
    picks, x, gain, qkv, outproj, upstream, upstream_one, normed_one, grad_one, att_one, gain_one,
    result, pieces, inverse, normed, grad_t, att_t, gain_sum, *scratch,
):
    keep, work = (*scratch[:5], att_t), scratch[5:]
    gain_sum[...] = gain_one[...]
    norm_rows(x, gain, normed, inverse)
    forward(picks[1], normed, qkv, keep)
    backward(x, gain, inverse, qkv, outproj, upstream, keep, work, grad_t, gain_sum, result)

    @pl.loop(0, 4)
    def _(q):
        weight_terms(
            q, (grad_one, grad_t), (normed_one, normed), (att_one, att_t),
            (upstream_one, upstream), gain_sum, pieces.at[q],
        )


def full(shape):
    return pl.BlockSpec(shape, lambda i, picks: (0,) * len(shape), pipeline_mode=pl.Buffered(1))


def chosen():
    return pl.BlockSpec((None, SEQ, D), lambda i, picks: (picks[0], 0, 0), pipeline_mode=pl.Buffered(1))


PARAMS = pltpu.CompilerParams(vmem_limit_bytes=48 * 2**20)
WEIGHTS = ((1, D), (D, QKV), (QW, D), (SEQ, D))
KEPT = ((SEQ, D), (QKV, SEQ), (QW, SEQ), (8, D))
KEPT_TYPES = (BF16, BF16, BF16, F32)


def slot_one(picks, acts, gain, qkv, outproj, upstream):
    return pl.pallas_call(
        first_kernel,
        grid_spec=pltpu.PrefetchScalarGridSpec(
            num_scalar_prefetch=1,
            grid=(1,),
            in_specs=[chosen(), *(full(s) for s in WEIGHTS)],
            out_specs=[full((SEQ, D)), *(full(s) for s in KEPT)],
            scratch_shapes=[INV, *KEEP, *WORK],
        ),
        out_shape=[
            jax.ShapeDtypeStruct((SEQ, D), BF16),
            *(jax.ShapeDtypeStruct(s, t) for s, t in zip(KEPT, KEPT_TYPES)),
        ],
        cost_estimate=pl.CostEstimate(flops=2 * 10**9, bytes_accessed=6 * 10**6, transcendentals=5 * 10**5),
        compiler_params=PARAMS,
    )(picks, acts, gain, qkv, outproj, upstream)


def slot_two(picks, acts, gain, qkv, outproj, upstream, upstream_one, kept):
    return pl.pallas_call(
        second_kernel,
        grid_spec=pltpu.PrefetchScalarGridSpec(
            num_scalar_prefetch=1,
            grid=(1,),
            in_specs=[chosen(), *(full(s) for s in WEIGHTS), full((SEQ, D)), *(full(s) for s in KEPT)],
            out_specs=[full((SEQ, D)), full((4, 2, PIECE, 128))],
            scratch_shapes=[
                INV,
                *(pltpu.VMEM(s, t) for s, t in zip(KEPT, KEPT_TYPES)),
                *KEEP,
                *WORK,
            ],
        ),
        out_shape=[
            jax.ShapeDtypeStruct((SEQ, D), BF16),
            jax.ShapeDtypeStruct((4, 2, PIECE, 128), BF16),
        ],
        cost_estimate=pl.CostEstimate(flops=3 * 10**9, bytes_accessed=10 * 10**6, transcendentals=5 * 10**5),
        compiler_params=PARAMS,
    )(picks, acts, gain, qkv, outproj, upstream, upstream_one, *kept)


def shards(
    act_down, act_up, grad_down, grad_up, seed_down, seed_up, gain_down, qkv_down, outproj_down,
    gain_up, qkv_up, outproj_up, doc_offsets, slot_order,
):
    count = lax.axis_size("section")
    section = lax.axis_index("section")
    order = slot_order[:, 0]
    offsets = jnp.take_along_axis(doc_offsets[:, 0, :, 0], order, axis=1)
    picks = jnp.stack([order, offsets], axis=2)
    up = (act_up[0], gain_up, qkv_up[0], outproj_up[0])
    down = (act_down[0], gain_down, qkv_down[0], outproj_down[0])
    up_one, *up_kept = slot_one(picks[1, 0], *up, grad_up[0])
    from_below = lax.ppermute(up_one, "section", [(s, s + 1) for s in range(count - 1)])
    down_one, *down_kept = slot_one(picks[0, 0], *down, grad_down[0])
    from_above = lax.ppermute(down_one, "section", [(s, s - 1) for s in range(1, count)])
    up_stream = jnp.where(section == 0, seed_up, from_below)
    down_stream = jnp.where(section == count - 1, seed_down, from_above)
    up_two, up_pieces = slot_two(picks[1, 1], *up, up_stream, grad_up[0], up_kept)
    up_sum = lax.psum_scatter(up_pieces.reshape(8, PIECE, 128), "dp", scatter_dimension=0, tiled=True)
    down_two, down_pieces = slot_two(picks[0, 1], *down, down_stream, grad_down[0], down_kept)
    down_sum = lax.psum_scatter(down_pieces.reshape(8, PIECE, 128), "dp", scatter_dimension=0, tiled=True)
    mirror = lax.ppermute(up_sum, "section", [(s, count - 1 - s) for s in range(count)])
    total = down_sum[0].astype(F32) + mirror[0].astype(F32)
    grad_qkv = total[:QKV].T
    grad_out = total[QKV : QKV + QW].reshape(8, HD, 128).transpose(1, 0, 2).reshape(HD, D)
    grad_gain = total[QKV + QW]
    input_grads = jnp.stack([jnp.stack([down_one, down_two]), jnp.stack([up_one, up_two])])[:, None]
    return input_grads, grad_gain[None], grad_qkv[None], grad_out[None]


def solution(mesh):
    return jax.shard_map(
        shards,
        mesh=mesh,
        in_specs=(
            P("section", None, "dp", None),
            P("section", None, "dp", None),
            P("section", "dp", None),
            P("section", "dp", None),
            P("dp", None),
            P("dp", None),
            P("section", None),
            P("section", None, None),
            P("section", None, None),
            P("section", None),
            P("section", None, None),
            P("section", None, None),
            P(None, "section", None, "dp"),
            P(None, "section", None),
        ),
        out_specs=(
            P(None, "section", None, "dp", None),
            P("section", "dp"),
            P("section", "dp", None),
            P("section", "dp", None),
        ),
        check_vma=False,
    )
```

profile of v0, /device:TPU:14, one launch (start us, length us, event | category | flops | bytes accessed | tf_op | source)
XLA Modules:
  0.0 196.4 jit_solution(15942410659337620991)
XLA Ops:
  9.4 1.1 fusion.5
  10.5 1.4 copy-done.1
  11.9 1.2 copy-done.3
  13.1 1.2 copy-done.5
  14.4 1.0 copy-done.10
  16.1 11.8 %shard_map.167 = (bf16[256,1024]{1,0:T(8,128)(2,1)S(1)}, bf16[256,1024]{1,0:T(8,128)(2,1)S(1)}, bf16[768,256]{1,0:T(8,128)(2,1)S(1)}, bf16[512,256]{1,0:T(8,128)(2,1)S(1)}, f32[8,1024]{1,0:T(8,128)S(1)}) custom-call(s32[2]{0:T(128)S(1)} %get-tuple-element.47.picks, bf16[2,256,1024]{2,1,0:T(8,128)(2,1)S(1)} %bitcast.46, f32[1,1024]{1,0:T(1,128)S(1)} %copy-done.14, ...), custom_call_target="tpu_custom_call" | custom-call | flops 2000000000 | bytes 6000000 | tf_op jit(solution)/shard_map/pallas_call | solution.py:199
  27.9 3.8 %collective-permute-start.1 = (bf16[256,1024]{1,0:T(8,128)(2,1)S(1)}, bf16[256,1024]{1,0:T(8,128)(2,1)}, u32[]{:S(2)}, u32[]{:S(2)}) collective-permute-start(bf16[256,1024]{1,0:T(8,128)(2,1)S(1)} %get-tuple-element.24), channel_id=1, source_target_pairs={{0,8},{8,16},{16,24},{24,32},{32,40},{40,48},{48,56},{56,64},{64,7... | collective-permute-start | bytes 1572872 | tf_op jit(solution)/shard_map/ppermute | solution.py:253
  31.8 12.7 %collective-permute-done.1 = bf16[256,1024]{1,0:T(8,128)(2,1)} collective-permute-done((bf16[256,1024]{1,0:T(8,128)(2,1)S(1)}, bf16[256,1024]{1,0:T(8,128)(2,1)}, u32[]{:S(2)}, u32[]{:S(2)}) %collective-permute-start.1) | collective-permute-done | bytes 524320 | tf_op jit(solution)/shard_map/ppermute | solution.py:253
  44.5 1.1 broadcast_select_fusion.upstream
  45.7 1.2 copy-done.6
  46.9 1.0 copy-done.18
  47.9 16.8 %shard_map.168 = (bf16[256,1024]{1,0:T(8,128)(2,1)S(1)}, bf16[4,2,1296,128]{3,2,1,0:T(8,128)(2,1)}) custom-call(s32[2]{0:T(128)S(1)} %get-tuple-element.46.picks, bf16[2,256,1024]{2,1,0:T(8,128)(2,1)S(1)} %bitcast.47, f32[1,1024]{1,0:T(1,128)S(1)} %copy-done.15, bf16[1024,768]{1,0:T(8,128)(2,1)} %bitcast.42, bf16[512,1024]{1,0:T(8,128)(2,1)S(1)} %bitcast.49, ...), custom_call_target="tpu_custom_call" | custom-call | flops 3000000000 | bytes 10000000 | tf_op jit(solution)/shard_map/pallas_call | solution.py:218
  64.8 1.1 copy-done.7
  66.0 1.4 copy-done.2
  67.4 1.2 copy-done.8
  68.6 1.0 copy-done.12
  69.6 11.8 %shard_map.165 = (bf16[256,1024]{1,0:T(8,128)(2,1)S(1)}, bf16[256,1024]{1,0:T(8,128)(2,1)S(1)}, bf16[768,256]{1,0:T(8,128)(2,1)S(1)}, bf16[512,256]{1,0:T(8,128)(2,1)S(1)}, f32[8,1024]{1,0:T(8,128)S(1)}) custom-call(s32[2]{0:T(128)S(1)} %get-tuple-element.44.picks, bf16[2,256,1024]{2,1,0:T(8,128)(2,1)S(1)} %bitcast.50, f32[1,1024]{1,0:T(1,128)S(1)} %copy-done.16, ...), custom_call_target="tpu_custom_call" | custom-call | flops 2000000000 | bytes 6000000 | tf_op jit(solution)/shard_map/pallas_call | solution.py:199
  81.5 0.8 copy-done.19
  82.3 3.2 %collective-permute-start = (bf16[256,1024]{1,0:T(8,128)(2,1)S(1)}, bf16[256,1024]{1,0:T(8,128)(2,1)}, u32[]{:S(2)}, u32[]{:S(2)}) collective-permute-start(bf16[256,1024]{1,0:T(8,128)(2,1)S(1)} %get-tuple-element.18), channel_id=1, source_target_pairs={{8,0},{16,8},{24,16},{32,24},{40,32},{48,40},{56,48},{64,56},{72,6... | collective-permute-start | bytes 1572872 | tf_op jit(solution)/shard_map/ppermute | solution.py:255
  85.4 24.2 %collective-permute-done = bf16[256,1024]{1,0:T(8,128)(2,1)} collective-permute-done((bf16[256,1024]{1,0:T(8,128)(2,1)S(1)}, bf16[256,1024]{1,0:T(8,128)(2,1)}, u32[]{:S(2)}, u32[]{:S(2)}) %collective-permute-start) | collective-permute-done | bytes 524320 | tf_op jit(solution)/shard_map/ppermute | solution.py:255
  109.6 1.1 broadcast_select_fusion.1.upstream
  110.8 1.2 copy-done.9
  112.0 1.0 copy-done.13
  113.0 1.0 copy-done.20
  114.1 0.9 copy-done.22
  115.0 0.8 copy-done.24
  115.8 16.9 %shard_map.166 = (bf16[256,1024]{1,0:T(8,128)(2,1)S(1)}, bf16[4,2,1296,128]{3,2,1,0:T(8,128)(2,1)}) custom-call(s32[2]{0:T(128)S(1)} %get-tuple-element.45.picks, bf16[2,256,1024]{2,1,0:T(8,128)(2,1)S(1)} %bitcast.51, f32[1,1024]{1,0:T(1,128)S(1)} %copy-done.16, bf16[1024,768]{1,0:T(8,128)(2,1)} %bitcast.44, bf16[512,1024]{1,0:T(8,128)(2,1)S(1)} %bitcast.53, ...), custom_call_target="tpu_custom_call" | custom-call | flops 3000000000 | bytes 10000000 | tf_op jit(solution)/shard_map/pallas_call | solution.py:218
  132.7 3.1 %collective-permute-start.2 = (bf16[1,1296,128]{2,1,0:T(8,128)(2,1)}, bf16[1,1296,128]{2,1,0:T(8,128)(2,1)S(1)}, u32[]{:S(2)}, u32[]{:S(2)}) collective-permute-start(bf16[1,1296,128]{2,1,0:T(8,128)(2,1)} %reduce-scatter.5.cloned.1.call-done), channel_id=1, source_target_pairs={{0,248},{8,240},{16,232},{24,224},{32,216},{40,208},{48,200},{56,1... | collective-permute-start | bytes 995336 | tf_op jit(solution)/shard_map/ppermute | solution.py:262
  136.0 1.5 maximum_bitcast_fusion
  137.5 48.6 %reduce-scatter.3.cloned.1.call-done = bf16[1,1296,128]{2,1,0:T(8,128)(2,1)} async-done(((bf16[8,1296,128]{2,1,0:T(8,128)(2,1)}), bf16[1,1296,128]{2,1,0:T(8,128)(2,1)}) %reduce-scatter.3.cloned.1.call-update) | async-done | bytes 331792 | tf_op jit(solution)/shard_map/reduce_scatter | solution.py:261
  186.1 1.0 convert_add_fusion
  188.6 0.9 copy.26
  (51 shorter events, 4.7 us)
Async XLA Ops:
  7.2 0.8 copy-start
  7.2 125.5 %reduce-scatter.5.cloned.1.call-start = ((), (), s32[]{:S(2)}) async-start(), calls=%async_computation.3 | async-start | bytes 2985984 | tf_op jit(solution)/shard_map/reduce_scatter | solution.py:259
  10.5 1.4 copy-start.1
  11.9 1.2 copy-start.3
  13.1 1.2 copy-start.5
  14.4 1.0 copy-start.10
  15.4 0.7 copy-start.14
  16.1 29.5 %copy-start.4 = (bf16[1,2,256,1024]{3,2,1,0:T(8,128)(2,1)S(1)}, bf16[1,2,256,1024]{3,2,1,0:T(8,128)(2,1)}, u32[]{:S(2)}) copy-start(bf16[1,2,256,1024]{3,2,1,0:T(8,128)(2,1)} %param.15) | copy-start | bytes 3145732
  16.1 29.5 %copy-start.11 = (bf16[1,256,1024]{2,1,0:T(8,128)(2,1)S(1)}, bf16[1,256,1024]{2,1,0:T(8,128)(2,1)}, u32[]{:S(2)}) copy-start(bf16[1,256,1024]{2,1,0:T(8,128)(2,1)} %param.17) | copy-start | bytes 1572868
  16.1 29.5 %copy-start.15 = (f32[1,1024]{1,0:T(1,128)S(1)}, f32[1,1024]{1,0:T(1,128)}, u32[]{:S(2)}) copy-start(f32[1,1024]{1,0:T(1,128)} %gain.7) | copy-start | bytes 12292
  27.9 17.7 %copy-start.17 = (bf16[256,1024]{1,0:T(8,128)(2,1)}, bf16[256,1024]{1,0:T(8,128)(2,1)S(1)}, u32[]{:S(2)}) copy-start(bf16[256,1024]{1,0:T(8,128)(2,1)S(1)} %get-tuple-element.25.normed_one) | copy-start | bytes 1572868
  27.9 16.6 %collective-permute-start.1 = (bf16[256,1024]{1,0:T(8,128)(2,1)S(1)}, bf16[256,1024]{1,0:T(8,128)(2,1)}, u32[]{:S(2)}, u32[]{:S(2)}) collective-permute-start(bf16[256,1024]{1,0:T(8,128)(2,1)S(1)} %get-tuple-element.24), channel_id=1, source_target_pairs={{0,8},{8,16},{16,24},{24,32},{32,40},{40,48},{48,56},{56,64},{64,7... | collective-permute-start | bytes 1572872 | tf_op jit(solution)/shard_map/ppermute | solution.py:253
  45.6 1.2 copy-start.6
  46.9 1.0 copy-start.18
  64.7 1.2 copy-start.7
  64.7 1.2 copy-start.16
  64.8 121.3 %reduce-scatter.3.cloned.1.call-start = ((), (), s32[]{:S(2)}) async-start(), calls=%async_computation.2 | async-start | bytes 2985984 | tf_op jit(solution)/shard_map/reduce_scatter | solution.py:261
  66.0 1.4 copy-start.2
  67.4 1.2 copy-start.8
  68.6 1.0 copy-start.12
  81.5 0.8 copy-start.19
  82.3 28.5 %copy-start.21 = (bf16[512,256]{1,0:T(8,128)(2,1)}, bf16[512,256]{1,0:T(8,128)(2,1)S(1)}, u32[]{:S(2)}) copy-start(bf16[512,256]{1,0:T(8,128)(2,1)S(1)} %get-tuple-element.21.att_one) | copy-start | bytes 786436
  82.3 28.5 %copy-start.23 = (f32[8,1024]{1,0:T(8,128)}, f32[8,1024]{1,0:T(8,128)S(1)}, u32[]{:S(2)}) copy-start(f32[8,1024]{1,0:T(8,128)S(1)} %get-tuple-element.22.gain_one) | copy-start | bytes 98308
  82.3 27.4 %collective-permute-start = (bf16[256,1024]{1,0:T(8,128)(2,1)S(1)}, bf16[256,1024]{1,0:T(8,128)(2,1)}, u32[]{:S(2)}, u32[]{:S(2)}) collective-permute-start(bf16[256,1024]{1,0:T(8,128)(2,1)S(1)} %get-tuple-element.18), channel_id=1, source_target_pairs={{8,0},{16,8},{24,16},{32,24},{40,32},{48,40},{56,48},{64,56},{72,6... | collective-permute-start | bytes 1572872 | tf_op jit(solution)/shard_map/ppermute | solution.py:255
  110.8 1.2 copy-start.9
  112.0 1.0 copy-start.13
  113.0 1.0 copy-start.20
  114.1 1.0 copy-start.22
  115.0 0.8 copy-start.24
  132.7 53.4 %collective-permute-start.2 = (bf16[1,1296,128]{2,1,0:T(8,128)(2,1)}, bf16[1,1296,128]{2,1,0:T(8,128)(2,1)S(1)}, u32[]{:S(2)}, u32[]{:S(2)}) collective-permute-start(bf16[1,1296,128]{2,1,0:T(8,128)(2,1)} %reduce-scatter.5.cloned.1.call-done), channel_id=1, source_target_pairs={{0,248},{8,240},{16,232},{24,224},{32,216},{40,208},{48,200},{56,1... | collective-permute-start | bytes 995336 | tf_op jit(solution)/shard_map/ppermute | solution.py:262
Sparse Core Ops, SparseCore 0:
  64.9 57.3 reduce-scatter.4
  132.8 53.2 reduce-scatter.2
where the time goes:
time: 197 us; the launch traced here: 196 us
  waiting for transfers between devices  85.5 us (43%)
  Pallas kernels  57.3 us (29%)
  local copies, waits for them, and re-layouts  21.7 us (11%)
  between operations  14.2 us (7%)
  starting transfers between devices  10.2 us (5%)
  other arithmetic  7.39 us (4%)
    reduce_scatter x1, waiting for transfers between devices, shards(): lax.psum_scatter(down_pieces.reshape(8, PIECE, 128), 'dp', scatter_dimens...  48.6 us
    pallas_call x2, Pallas kernels, slot_two(): pl.pallas_call(second_kernel, grid_spec=pltpu.PrefetchScalarGridSpec(num_...  33.7 us
    ppermute x1, waiting for transfers between devices, shards(): lax.ppermute(down_one, 'section', [(s, s - 1) for s in range(1, count)])  24.2 us
    pallas_call x2, Pallas kernels, slot_one(): pl.pallas_call(first_kernel, grid_spec=pltpu.PrefetchScalarGridSpec(num_s...  23.6 us
    unnamed x51, local copies, waits for them, and re-layouts  19.4 us
    ppermute x1, waiting for transfers between devices, shards(): lax.ppermute(up_one, 'section', [(s, s + 1) for s in range(count - 1)])  12.7 us
  transfers between devices with their start and end apart: 5, of which 3 were waited for; matrix products, arithmetic and copies ran while one was open for 1% of the time, Pallas kernels for 15%

commit v1 on v0

v1 whole, which is shorter than its diff:
```python
import functools

import jax
import jax.numpy as jnp
from jax import lax
from jax.experimental import pallas as pl
from jax.experimental.pallas import tpu as pltpu
from jax.sharding import PartitionSpec as P

F32, BF16 = jnp.float32, jnp.bfloat16
EPSILON = 1e-05
D, SEQ, HEADS, GROUP, HD = 1024, 256, 8, 4, 64
QW, QKV = 512, 768
ROWS = 32
PIECE = QKV + QW + 16
SPLIT = 640
HALVES = (slice(0, SPLIT), slice(SPLIT, PIECE))
MESH = pl.DeviceIdType.MESH


def nn(a, b):
    return jnp.dot(a, b, preferred_element_type=F32)


def nt(a, b):
    return lax.dot_general(a, b, (((1,), (1,)), ((), ())), preferred_element_type=F32)


def norm_rows(x, gain, normed, inverse):
    for step in range(SEQ // ROWS):
        rows = slice(step * ROWS, step * ROWS + ROWS)
        xf = x(rows)
        inv = lax.rsqrt(jnp.mean(xf * xf, axis=1, keepdims=True) + EPSILON)
        normed[rows, :] = (xf * inv * gain[...]).astype(BF16)
        inverse[rows, :] = jnp.broadcast_to(inv, (ROWS, 128))


def forward(offset, normed, qkv, keep):
    proj_t, keys, values, soft, soft_low, att_t = keep
    for n in range(3):
        cols = slice(n * 256, n * 256 + 256)
        part = nn(normed[...], qkv[:, cols])
        proj_t[cols, :] = part.T.astype(BF16)
        if n == 2:
            low = part.astype(BF16)
            keys[0], keys[1] = low[:, :64], low[:, 64:128]
            values[0], values[1] = low[:, 128:192], low[:, 192:256]
    for head in range(HEADS):
        group = head // GROUP
        rows = slice(head * HD, head * HD + HD)
        scores = nn(keys[group], proj_t[rows, :])
        for half, depth in ((0, 128), (1, 256)):
            cols = slice(half * 128, half * 128 + 128)
            at_key = lax.broadcasted_iota(jnp.int32, (depth, 128), 0)
            at_query = lax.broadcasted_iota(jnp.int32, (depth, 128), 1) + half * 128
            allowed = (at_key <= at_query) & ((at_query < offset) | (at_key >= offset))
            part = jnp.where(allowed, scores[:depth, cols] * (HD**-0.5), -1e30)
            raised = jnp.exp(part - jnp.max(part, axis=0, keepdims=True))
            weights = raised * (1.0 / jnp.sum(raised, axis=0, keepdims=True))
            soft[head, :depth, cols] = weights
            soft_low[head, :depth, cols] = weights.astype(BF16)
        soft_low[head, 128:, :128] = jnp.zeros((128, 128), BF16)
        value_rows = slice(QW + 128 + group * HD, QW + 128 + group * HD + HD)
        att_t[rows, :] = nn(proj_t[value_rows, :], soft_low[head]).astype(BF16)


def backward(x, gain, inverse, qkv, outproj, upstream, keep, work, grad_t, gain_sum, result, midway=None):
    proj_t, keys, values, soft, soft_low, _ = keep
    att_grad, score_grad, grad, normed_grad = work
    for m in range(2):
        rows = slice(m * 256, m * 256 + 256)
        att_grad[rows, :] = nt(outproj[rows, :], upstream[...]).astype(BF16)
    for group in range(HEADS // GROUP):
        key_sum = jnp.zeros((HD, SEQ), F32)
        value_sum = jnp.zeros((HD, SEQ), F32)
        key_rows = slice(QW + group * HD, QW + group * HD + HD)
        value_rows = slice(QW + 128 + group * HD, QW + 128 + group * HD + HD)
        for head in range(group * GROUP, group * GROUP + GROUP):
            rows = slice(head * HD, head * HD + HD)
            low = att_grad[rows, :]
            soft_grad = nn(values[group], low)
            for half, depth in ((0, 128), (1, 256)):
                cols = slice(half * 128, half * 128 + 128)
                weights = soft[head, :depth, cols]
                part = soft_grad[:depth, cols]
                total = jnp.sum(weights * part, axis=0, keepdims=True)
                score_grad[head, :depth, cols] = (weights * (part - total) * (HD**-0.5)).astype(BF16)
            score_grad[head, 128:, :128] = jnp.zeros((128, 128), BF16)
            grad_t[rows, :] = nn(proj_t[key_rows, :], score_grad[head]).astype(BF16)
            key_sum = key_sum + nt(proj_t[rows, :], score_grad[head])
            value_sum = value_sum + nt(low, soft_low[head])
        grad_t[key_rows, :] = key_sum.astype(BF16)
        grad_t[value_rows, :] = value_sum.astype(BF16)
    if midway is not None:
        midway()
    for n in range(3):
        cols = slice(n * 256, n * 256 + 256)
        grad[:, cols] = grad_t[cols, :].T
    for n in range(4):
        cols = slice(n * 256, n * 256 + 256)
        normed_grad[:, cols] = nt(grad[...], qkv[cols, :])
    for step in range(SEQ // ROWS):
        rows = slice(step * ROWS, step * ROWS + ROWS)
        inv = inverse[rows, :][:, :1]
        scaled = x(rows) * inv
        hat = normed_grad[rows, :]
        both = hat * scaled
        partial = both[:8]
        for k in range(1, ROWS // 8):
            partial = partial + both[k * 8 : k * 8 + 8]
        gain_sum[...] += partial
        mean = jnp.mean(both * gain[...], axis=1, keepdims=True)
        moved = inv * (hat * gain[...] - scaled * mean)
        result[rows, :] = (upstream[rows, :].astype(F32) + moved).astype(BF16)


def weight_terms(q, grad_t, normed, att_t, upstream, gain_sum, piece):
    cols = pl.ds(pl.multiple_of(q * 256, 256), 256)
    for m in range(3):
        rows = slice(m * 256, m * 256 + 256)
        part = nn(grad_t[0][rows, :], normed[0][:, cols]) + nn(grad_t[1][rows, :], normed[1][:, cols])
        for core in range(2):
            piece[core, rows, :] = part[:, core * 128 : core * 128 + 128].astype(BF16)
    heads = pl.ds(pl.multiple_of(q * 128, 128), 128)
    for n in range(4):
        wide = slice(n * 256, n * 256 + 256)
        part = nn(att_t[0][heads, :], upstream[0][:, wide]) + nn(att_t[1][heads, :], upstream[1][:, wide])
        for core in range(2):
            for k in range(2):
                at = QKV + (2 * n + k) * HD
                block = part[core * HD : core * HD + HD, k * 128 : k * 128 + 128]
                piece[core, at : at + HD, :] = block.astype(BF16)
    for core in range(2):
        lanes = pl.ds(pl.multiple_of(q * 256 + core * 128, 128), 128)
        row = jnp.sum(gain_sum[:, lanes], axis=0, keepdims=True)
        piece[core, QKV + QW :, :] = jnp.broadcast_to(row, (16, 128)).astype(BF16)


SCRATCH = {
    "acts": pltpu.VMEM((2, 2, SEQ, D), BF16),
    "tops": pltpu.VMEM((2, SEQ, D), BF16),
    "seeds": pltpu.VMEM((2, SEQ, D), BF16),
    "gains": pltpu.VMEM((2, 1, D), F32),
    "qkvs": pltpu.VMEM((2, D, QKV), BF16),
    "outs": pltpu.VMEM((2, QW, D), BF16),
    "taken": pltpu.VMEM((2, SEQ, D), BF16),
    "grads": pltpu.VMEM((2, 2, SEQ, D), BF16),
    "normed": pltpu.VMEM((2, 2, SEQ, D), BF16),
    "grad_t": pltpu.VMEM((2, 2, QKV, SEQ), BF16),
    "att_t": pltpu.VMEM((2, 2, QW, SEQ), BF16),
    "gain_sum": pltpu.VMEM((2, 8, D), F32),
    "inverse": pltpu.VMEM((2, SEQ, 128), F32),
    "proj_t": pltpu.VMEM((2, QKV, SEQ), BF16),
    "keys": pltpu.VMEM((2, 2, SEQ, HD), BF16),
    "values": pltpu.VMEM((2, 2, SEQ, HD), BF16),
    "soft": pltpu.VMEM((2, HEADS, SEQ, SEQ), F32),
    "soft_low": pltpu.VMEM((2, HEADS, SEQ, SEQ), BF16),
    "att_grad": pltpu.VMEM((QW, SEQ), BF16),
    "score_grad": pltpu.VMEM((HEADS, SEQ, SEQ), BF16),
    "grad": pltpu.VMEM((SEQ, QKV), BF16),
    "normed_grad": pltpu.VMEM((SEQ, D), F32),
    "pieces": pltpu.VMEM((2, 4, 2, PIECE, 128), BF16),
    "paired": pltpu.VMEM((2, 4, PIECE, 128), BF16),
    "own": pltpu.VMEM((2, 4, PIECE, 128), BF16),
    "mirror": pltpu.VMEM((4, PIECE, 128), BF16),
    "ring": pltpu.VMEM((2, 4, PIECE, 128), BF16),
    "load_sem": pltpu.SemaphoreType.DMA((6, 2)),
    "save_sem": pltpu.SemaphoreType.DMA((2, 2)),
    "shift_sem": pltpu.SemaphoreType.DMA((2, 2)),
    "pair_sem": pltpu.SemaphoreType.DMA((2, 2, 4)),
    "mirror_sem": pltpu.SemaphoreType.DMA((2, 4, 2)),
    "ring_sem": pltpu.SemaphoreType.DMA((2, 2, 4, 2)),
}
LOADS = ("acts", "tops", "gains", "qkvs", "outs", "seeds")
AHEAD = ((0, 0), (1, 3), (0, 3))
BEHIND = ((0, 1), (1, 1), (0, 2))


def window(*refs):
    orders, offsets = refs[:2]
    sources = refs[2:14]
    input_grads, grad_gain, grad_qkv, grad_out = refs[14:18]
    s = dict(zip(SCRATCH, refs[18:]))

    section, replica = lax.axis_index("section"), lax.axis_index("dp")
    sections, replicas = lax.axis_size("section"), lax.axis_size("dp")
    low, core = section % 2, replica % 2
    height = (replica // 2) * 2 + low
    partner = (section, replica + 1 - 2 * core)
    across = (sections - 2 - section + 2 * low, replica)
    above = (section + 1 - 2 * low, (replica + 2 * low) % replicas)
    below = (section + 1 - 2 * low, (replica + replicas - 2 + 2 * low) % replicas)
    later = ((section + 1) % sections, replica)
    sooner = ((section + sections - 1) % sections, replica)

    barrier = pltpu.get_barrier_semaphore()
    for peer in (partner, across, above, below, later, sooner):
        pl.semaphore_signal(barrier, inc=1, device_id=peer, device_id_type=MESH)

    def load(name, c):
        where = LOADS.index(name)
        return pltpu.make_async_copy(sources[2 * where + c], s[name].at[pl.ds(c, 1)], s["load_sem"].at[where, c])

    for c in range(2):
        for name in ("acts", "gains", "qkvs", "outs", "tops"):
            load(name, c).start()
    for c in range(2):
        load("seeds", c).start()

    def loaded(name, c):
        where = s[name].at[pl.ds(c, 1)]
        pltpu.make_async_copy(where, where, s["load_sem"].at[LOADS.index(name), c]).wait()

    def picked(c, slot):
        chosen = orders[(1 - c) * 2 + slot]
        offset = jnp.where(chosen == 0, offsets[(1 - c) * 2], offsets[(1 - c) * 2 + 1])

        def rows_of(rows):
            return jnp.where(chosen == 0, s["acts"][c, 0, rows, :].astype(F32), s["acts"][c, 1, rows, :].astype(F32))

        return rows_of, offset

    def keep(c, slot):
        names = ("proj_t", "keys", "values", "soft", "soft_low")
        return (*(s[name].at[c] for name in names), s["att_t"].at[c, slot])

    def run_forward(c, slot):
        x, offset = picked(c, slot)
        norm_rows(x, s["gains"].at[c], s["normed"].at[c, slot], s["inverse"].at[c])
        forward(offset, s["normed"].at[c, slot], s["qkvs"].at[c], keep(c, slot))

    def run_backward(c, slot, upstream, midway=None):
        work = tuple(s[name] for name in ("att_grad", "score_grad", "grad", "normed_grad"))
        backward(
            picked(c, slot)[0], s["gains"].at[c], s["inverse"].at[c], s["qkvs"].at[c], s["outs"].at[c],
            upstream, keep(c, slot), work, s["grad_t"].at[c, slot], s["gain_sum"].at[c],
            s["grads"].at[c, slot], midway,
        )

    def save(c, slot):
        return pltpu.make_async_copy(
            s["grads"].at[c, slot], input_grads.at[1 - c, 0, slot], s["save_sem"].at[c, slot]
        )

    def remote(source, target, sems, device):
        return pltpu.make_async_remote_copy(
            src_ref=source, dst_ref=target, send_sem=sems[0], recv_sem=sems[1],
            device_id=device, device_id_type=MESH,
        )

    def shift(c):
        peer = ((section + sections + 1 - 2 * c) % sections, replica)
        sems = (s["shift_sem"].at[0, c], s["shift_sem"].at[1, c])
        return remote(s["grads"].at[c, 0], s["taken"].at[c], sems, peer)

    def pair(c, j):
        sems = (s["pair_sem"].at[0, c, j], s["pair_sem"].at[1, c, j])
        return remote(s["pieces"].at[c, j, 1 - core], s["paired"].at[c, j], sems, partner)

    def fold(j, h):
        sems = (s["mirror_sem"].at[0, j, h], s["mirror_sem"].at[1, j, h])
        return remote(s["own"].at[0, j, HALVES[h]], s["mirror"].at[j, HALVES[h]], sems, across)

    def add_pair(c, j, rows):
        total = s["pieces"][c, j, core, rows, :].astype(F32) + s["paired"][c, j, rows, :].astype(F32)
        s["own"][c, j, rows, :] = total.astype(BF16)

    def send_mirror():
        for j in (0, 1, 3, 2):
            pair(0, j).wait_recv()
            for h in range(2):
                add_pair(0, j, HALVES[h])
        for first, second in ((0, 1), (3, 2)):
            for j, h in ((first, 1), (second, 0), (first, 0), (second, 1)):
                fold(j, h).start()

    s["gain_sum"][...] = jnp.zeros_like(s["gain_sum"])

    @pl.loop(0, 2)
    def _(c):
        for name in ("acts", "gains", "qkvs"):
            loaded(name, c)
        run_forward(c, 0)
        loaded("outs", c)
        loaded("tops", c)
        run_backward(c, 0, s["tops"].at[c])

        @pl.when(c == 0)
        def _():
            pl.semaphore_wait(barrier, 6)

        shift(c).start()
        save(c, 0).start()

    @pl.loop(0, 2)
    def _(c):
        run_forward(c, 1)

    @pl.loop(0, 2)
    def _(c):
        loaded("seeds", c)
        shift(c).wait_recv()

        @pl.when(section == (sections - 1) * c)
        def _():
            s["taken"][c] = s["seeds"][c]

        def midway():
            @pl.when(c == 1)
            def _():
                send_mirror()

        run_backward(c, 1, s["taken"].at[c], midway)
        save(c, 1).start()

        @pl.loop(0, 4)
        def _(j):
            weight_terms(
                ((height + 3 + c + 2 * j) % replicas) // 2,
                [s["grad_t"].at[c, k] for k in range(2)],
                [s["normed"].at[c, k] for k in range(2)],
                [s["att_t"].at[c, k] for k in range(2)],
                [s["tops"].at[c], s["taken"].at[c]],
                s["gain_sum"].at[c],
                s["pieces"].at[c, j],
            )
            pair(c, j).start()

    ways = (above, below)

    def term(way, step):
        if step == 0:
            return s["own"].at[1, 0]
        mirrored, j = (AHEAD, BEHIND)[way][step - 1]
        return s["mirror"].at[j] if mirrored == 0 else s["own"].at[1, j]

    def hop(way, step, h):
        sems = (s["ring_sem"].at[0, way, step, h], s["ring_sem"].at[1, way, step, h])
        return remote(term(way, step).at[HALVES[h]], s["ring"].at[way, step, HALVES[h]], sems, ways[way])

    def forward_on(way, step, h):
        rows = HALVES[h]
        if step > 0:
            mirrored, j = (AHEAD, BEHIND)[way][step - 1]
            if mirrored == 0:
                fold(j, h).wait_recv()
            if step > 1 or h == way:
                hop(way, step - 1, h).wait_recv()
                mine = term(way, step)
                total = mine[rows, :].astype(F32) + s["ring"][way, step - 1, rows, :].astype(F32)
                mine[rows, :] = total.astype(BF16)
        hop(way, step, h).start()

    pair(1, 0).wait_recv()
    for h in range(2):
        add_pair(1, 0, HALVES[h])
        forward_on(h, 0, h)
    for j in (3, 1, 2):
        pair(1, j).wait_recv()
        for h in range(2):
            add_pair(1, j, HALVES[h])
    for step in range(1, 4):
        for turn in range(2):
            for way in range(2):
                forward_on(way, step, (1 - way) if turn == 0 else way)
    for way in range(2):
        for h in range(2):
            hop(way, 3, h).wait_recv()

    total = s["own"][1, 2].astype(F32) + s["ring"][0, 3].astype(F32) + s["ring"][1, 3].astype(F32)
    for n in range(3):
        grad_qkv[0, :, n * 256 : n * 256 + 256] = total[n * 256 : n * 256 + 256, :].T
    for k in range(8):
        grad_out[0, :, k * 128 : k * 128 + 128] = total[QKV + k * HD : QKV + k * HD + HD, :]
    grad_gain[...] = total[QKV + QW : QKV + QW + 1, :]

    for c in range(2):
        shift(c).wait_send()
        for slot in range(2):
            save(c, slot).wait()
        for j in range(4):
            pair(c, j).wait_send()
    for j in range(4):
        for h in range(2):
            fold(j, h).wait_send()
    for way in range(2):
        hop(way, 0, way).wait_send()
        for step in range(1, 4):
            for h in range(2):
                hop(way, step, h).wait_send()


def shards(
    act_down, act_up, grad_down, grad_up, seed_down, seed_up, gain_down, qkv_down, outproj_down,
    gain_up, qkv_up, outproj_up, doc_offsets, slot_order,
):
    shapes = (
        jax.ShapeDtypeStruct((2, 1, 2, SEQ, D), BF16),
        jax.ShapeDtypeStruct((1, 128), F32),
        jax.ShapeDtypeStruct((1, 128, QKV), F32),
        jax.ShapeDtypeStruct((1, HD, D), F32),
    )
    whole = pl.BlockSpec(memory_space=pltpu.VMEM)
    anywhere = pl.BlockSpec(memory_space=pl.ANY)
    numbers = pl.BlockSpec(memory_space=pltpu.SMEM)
    return pl.pallas_call(
        window,
        in_specs=[numbers] * 2 + [anywhere] * 12,
        out_specs=[anywhere, whole, whole, whole],
        out_shape=shapes,
        scratch_shapes=list(SCRATCH.values()),
        compiler_params=pltpu.CompilerParams(
            vmem_limit_bytes=60 * 2**20, collective_id=0, has_side_effects=True
        ),
    )(
        slot_order.reshape(4), doc_offsets.reshape(4), act_up, act_down, grad_up, grad_down,
        gain_up[None], gain_down[None], qkv_up, qkv_down, outproj_up, outproj_down, seed_up[None], seed_down[None],
    )


def solution(mesh):
    return jax.shard_map(
        shards,
        mesh=mesh,
        in_specs=(
            P("section", None, "dp", None),
            P("section", None, "dp", None),
            P("section", "dp", None),
            P("section", "dp", None),
            P("dp", None),
            P("dp", None),
            P("section", None),
            P("section", None, None),
            P("section", None, None),
            P("section", None),
            P("section", None, None),
            P("section", None, None),
            P(None, "section", None, "dp"),
            P(None, "section", None),
        ),
        out_specs=(
            P(None, "section", None, "dp", None),
            P("section", "dp"),
            P("section", "dp", None),
            P("section", "dp", None),
        ),
        check_vma=False,
    )
```

time: 197 us -> 90.2 us (0.46)
  the two profiles are of different devices: /device:TPU:14 before, /device:TPU:66 now
where the time goes in v1:
time: 90.2 us; the launch traced here: 88.6 us
  Pallas kernels  78.4 us (87%)
  local copies, waits for them, and re-layouts  6.81 us (8%)
  other arithmetic  2.68 us (3%)
    pallas_call x1, Pallas kernels, shards(): pl.pallas_call(window, in_specs=[numbers] * 2 + [anywhere] * 12, out_spec...  78.4 us
    unnamed x11, local copies, waits for them, and re-layouts  5.63 us
    unnamed x2, other arithmetic  2.68 us

profile of v1, /device:TPU:66, one launch (start us, length us, event | category | flops | bytes accessed | tf_op | source)
XLA Modules:
  0.0 88.6 jit_solution(12222931812070333675)
XLA Ops:
  0.6 0.5 broadcast.6
  1.1 1.3 %reduce.7 = s32[2,2]{1,0:T(2,128)S(1)} reduce(s32[2,1,2,1]{2,3,1,0:T(1,128)} %param.26, s32[]{:T(128)} %broadcast.6), dimensions={1,3}, to_apply=%param.26.reduce_sub_computation.3 | reduce | bytes 36 | tf_op args[12]
  2.5 0.6 reshape.15.refs_1_
  3.1 1.3 %reduce.6 = s32[2,2]{1,0:T(2,128)S(1)} reduce(s32[2,1,2]{2,1,0:T(1,128)} %param.27, s32[]{:T(128)} %broadcast.6), dimensions={1}, to_apply=%param.27.reduce_sub_computation.3 | reduce | bytes 36 | tf_op args[13]
  4.4 0.6 reshape.14.refs_0_
  5.0 78.4 %shard_map.165 = (bf16[2,1,2,256,1024]{4,3,2,1,0:T(8,128)(2,1)}, f32[1,128]{1,0:T(1,128)}, f32[1,128,768]{2,1,0:T(8,128)}, f32[1,64,1024]{2,1,0:T(8,128)}) custom-call(s32[4]{0:T(128)} %reshape.14.refs_0_, s32[4]{0:T(128)} %reshape.15.refs_1_, bf16[1,2,256,1024]{3,2,1,0:T(8,128)(2,1)} %refs_2_.1, bf16[1,2,256,1024]{3,2,1,0:T(8,128)(2,1)} %refs_3_.1, ...), custom_call_target="tpu_custom_call" | custom-call | tf_op jit(solution)/shard_map/pallas_call | solution.py:406
  83.4 0.0 copy-start.2
  83.5 0.0 copy-start
  83.5 0.0 copy-start.1
  83.5 3.1 %copy.22 = bf16[2,1,2,256,1024]{4,3,2,1,0:T(8,128)(2,1)} copy(bf16[2,1,2,256,1024]{4,3,2,1,0:T(8,128)(2,1)} %get-tuple-element.8) | data formatting | bytes 4194304
  86.6 0.0 copy-done.2
  86.6 0.5 copy.23
  87.1 0.0 copy-done
  87.1 0.7 copy.24
  87.9 0.0 copy-done.1
  87.9 0.7 copy.25
Async XLA Ops:
  83.4 3.2 %copy-start.2 = (f32[1,128]{1,0:T(1,128)S(1)}, f32[1,128]{1,0:T(1,128)}, u32[]{:S(2)}) copy-start(f32[1,128]{1,0:T(1,128)} %get-tuple-element.9) | copy-start | bytes 1540
  83.5 3.7 %copy-start = (f32[1,128,768]{2,1,0:T(8,128)S(1)}, f32[1,128,768]{2,1,0:T(8,128)}, u32[]{:S(2)}) copy-start(f32[1,128,768]{2,1,0:T(8,128)} %get-tuple-element.10) | copy-start | bytes 1179652
  83.5 4.4 %copy-start.1 = (f32[1,64,1024]{2,1,0:T(8,128)S(1)}, f32[1,64,1024]{2,1,0:T(8,128)}, u32[]{:S(2)}) copy-start(f32[1,64,1024]{2,1,0:T(8,128)} %get-tuple-element.11) | copy-start | bytes 786436

commit v2 on v1

v2 whole, which is shorter than its diff:
```python
import functools

import jax
import jax.numpy as jnp
from jax import lax
from jax.experimental import pallas as pl
from jax.experimental.pallas import tpu as pltpu
from jax.sharding import PartitionSpec as P

F32, BF16 = jnp.float32, jnp.bfloat16
EPSILON = 1e-05
D, SEQ, HEADS, GROUP, HD = 1024, 256, 8, 4, 64
QW, QKV = 512, 768
ROWS = 32
PIECE = QKV + QW + 16
BLOCKS = (slice(0, QW), slice(QW, PIECE))
FOLDS = (slice(0, QW), slice(QW, 896), slice(896, PIECE))
PARTS = (slice(0, 256), slice(256, QW), slice(QW, 896), slice(896, PIECE))
FOLD_OF = (0, 0, 1, 2)
MESH = pl.DeviceIdType.MESH


def nn(a, b):
    return jnp.dot(a, b, preferred_element_type=F32)


def nt(a, b):
    return lax.dot_general(a, b, (((1,), (1,)), ((), ())), preferred_element_type=F32)


def norm_rows(x, gain, normed, inverse):
    for step in range(SEQ // ROWS):
        rows = slice(step * ROWS, step * ROWS + ROWS)
        xf = x(rows)
        inv = lax.rsqrt(jnp.mean(xf * xf, axis=1, keepdims=True) + EPSILON)
        normed[rows, :] = (xf * inv * gain[...]).astype(BF16)
        inverse[rows, :] = jnp.broadcast_to(inv, (ROWS, 128))


def forward(offset, normed, qkv, keep):
    proj_t, keys, values, soft, soft_low, att_t = keep
    for n in range(3):
        cols = slice(n * 256, n * 256 + 256)
        part = nn(normed[...], qkv[:, cols])
        proj_t[cols, :] = part.T.astype(BF16)
        if n == 2:
            low = part.astype(BF16)
            keys[0], keys[1] = low[:, :64], low[:, 64:128]
            values[0], values[1] = low[:, 128:192], low[:, 192:256]
    for head in range(HEADS):
        group = head // GROUP
        rows = slice(head * HD, head * HD + HD)
        scores = nn(keys[group], proj_t[rows, :])
        for half, depth in ((0, 128), (1, 256)):
            cols = slice(half * 128, half * 128 + 128)
            at_key = lax.broadcasted_iota(jnp.int32, (depth, 128), 0)
            at_query = lax.broadcasted_iota(jnp.int32, (depth, 128), 1) + half * 128
            allowed = (at_key <= at_query) & ((at_query < offset) | (at_key >= offset))
            part = jnp.where(allowed, scores[:depth, cols] * (HD**-0.5), -1e30)
            raised = jnp.exp(part - jnp.max(part, axis=0, keepdims=True))
            weights = raised * (1.0 / jnp.sum(raised, axis=0, keepdims=True))
            soft[head, :depth, cols] = weights
            soft_low[head, :depth, cols] = weights.astype(BF16)
        soft_low[head, 128:, :128] = jnp.zeros((128, 128), BF16)
        value_rows = slice(QW + 128 + group * HD, QW + 128 + group * HD + HD)
        att_t[rows, :] = nn(proj_t[value_rows, :], soft_low[head]).astype(BF16)


def backward(x, gain, inverse, qkv, outproj, upstream, keep, work, grad_t, gain_sum, result, hooks=()):
    hooks = dict(hooks)
    proj_t, keys, values, soft, soft_low, _ = keep
    att_grad, score_grad, grad, normed_grad = work
    for m in range(2):
        rows = slice(m * 256, m * 256 + 256)
        att_grad[rows, :] = nt(outproj[rows, :], upstream[...]).astype(BF16)
    if "start" in hooks:
        hooks["start"]()
    for group in range(HEADS // GROUP):
        key_sum = jnp.zeros((HD, SEQ), F32)
        value_sum = jnp.zeros((HD, SEQ), F32)
        key_rows = slice(QW + group * HD, QW + group * HD + HD)
        value_rows = slice(QW + 128 + group * HD, QW + 128 + group * HD + HD)
        for head in range(group * GROUP, group * GROUP + GROUP):
            rows = slice(head * HD, head * HD + HD)
            low = att_grad[rows, :]
            soft_grad = nn(values[group], low)
            for half, depth in ((0, 128), (1, 256)):
                cols = slice(half * 128, half * 128 + 128)
                weights = soft[head, :depth, cols]
                part = soft_grad[:depth, cols]
                total = jnp.sum(weights * part, axis=0, keepdims=True)
                score_grad[head, :depth, cols] = (weights * (part - total) * (HD**-0.5)).astype(BF16)
            score_grad[head, 128:, :128] = jnp.zeros((128, 128), BF16)
            grad_t[rows, :] = nn(proj_t[key_rows, :], score_grad[head]).astype(BF16)
            key_sum = key_sum + nt(proj_t[rows, :], score_grad[head])
            value_sum = value_sum + nt(low, soft_low[head])
        grad_t[key_rows, :] = key_sum.astype(BF16)
        grad_t[value_rows, :] = value_sum.astype(BF16)
        if group in hooks:
            hooks[group]()
    for n in range(3):
        cols = slice(n * 256, n * 256 + 256)
        grad[:, cols] = grad_t[cols, :].T
    for n in range(4):
        cols = slice(n * 256, n * 256 + 256)
        normed_grad[:, cols] = nt(grad[...], qkv[cols, :])
    for step in range(SEQ // ROWS):
        rows = slice(step * ROWS, step * ROWS + ROWS)
        inv = inverse[rows, :][:, :1]
        scaled = x(rows) * inv
        hat = normed_grad[rows, :]
        both = hat * scaled
        partial = both[:8]
        for k in range(1, ROWS // 8):
            partial = partial + both[k * 8 : k * 8 + 8]
        gain_sum[...] += partial
        mean = jnp.mean(both * gain[...], axis=1, keepdims=True)
        moved = inv * (hat * gain[...] - scaled * mean)
        result[rows, :] = (upstream[rows, :].astype(F32) + moved).astype(BF16)


def out_terms(q, att_t, upstream, piece):
    heads = pl.ds(pl.multiple_of(q * 128, 128), 128)
    for n in range(4):
        wide = slice(n * 256, n * 256 + 256)
        part = nn(att_t[0][heads, :], upstream[0][:, wide]) + nn(att_t[1][heads, :], upstream[1][:, wide])
        for core in range(2):
            for k in range(2):
                at = (2 * n + k) * HD
                block = part[core * HD : core * HD + HD, k * 128 : k * 128 + 128]
                piece[core, at : at + HD, :] = block.astype(BF16)


def qkv_terms(q, grad_t, normed, gain_sum, piece):
    cols = pl.ds(pl.multiple_of(q * 256, 256), 256)
    for m in range(3):
        rows = slice(m * 256, m * 256 + 256)
        part = nn(grad_t[0][rows, :], normed[0][:, cols]) + nn(grad_t[1][rows, :], normed[1][:, cols])
        for core in range(2):
            at = QW + m * 256
            piece[core, at : at + 256, :] = part[:, core * 128 : core * 128 + 128].astype(BF16)
    for core in range(2):
        lanes = pl.ds(pl.multiple_of(q * 256 + core * 128, 128), 128)
        row = jnp.sum(gain_sum[:, lanes], axis=0, keepdims=True)
        piece[core, QW + QKV :, :] = jnp.broadcast_to(row, (16, 128)).astype(BF16)


SCRATCH = {
    "orders": pltpu.SMEM((2, 1, 2), jnp.int32),
    "offsets": pltpu.SMEM((2, 1, 1, 2), jnp.int32),
    "number_sem": pltpu.SemaphoreType.DMA((2,)),
    "acts": pltpu.VMEM((2, 2, SEQ, D), BF16),
    "tops": pltpu.VMEM((2, SEQ, D), BF16),
    "seeds": pltpu.VMEM((2, SEQ, D), BF16),
    "gains": pltpu.VMEM((2, 1, D), F32),
    "qkvs": pltpu.VMEM((2, D, QKV), BF16),
    "outs": pltpu.VMEM((2, QW, D), BF16),
    "taken": pltpu.VMEM((2, SEQ, D), BF16),
    "normed": pltpu.VMEM((2, 2, SEQ, D), BF16),
    "grad_t": pltpu.VMEM((2, 2, QKV, SEQ), BF16),
    "att_t": pltpu.VMEM((2, 2, QW, SEQ), BF16),
    "gain_sum": pltpu.VMEM((2, 8, D), F32),
    "inverse": pltpu.VMEM((2, SEQ, 128), F32),
    "proj_t": pltpu.VMEM((2, QKV, SEQ), BF16),
    "keys": pltpu.VMEM((2, 2, SEQ, HD), BF16),
    "values": pltpu.VMEM((2, 2, SEQ, HD), BF16),
    "soft": pltpu.VMEM((2, HEADS, SEQ, SEQ), F32),
    "soft_low": pltpu.VMEM((2, HEADS, SEQ, SEQ), BF16),
    "att_grad": pltpu.VMEM((QW, SEQ), BF16),
    "score_grad": pltpu.VMEM((HEADS, SEQ, SEQ), BF16),
    "grad": pltpu.VMEM((SEQ, QKV), BF16),
    "normed_grad": pltpu.VMEM((SEQ, D), F32),
    "pieces": pltpu.VMEM((2, 4, 2, PIECE, 128), BF16),
    "paired": pltpu.VMEM((2, 4, PIECE, 128), BF16),
    "own": pltpu.VMEM((2, 4, PIECE, 128), BF16),
    "mirror": pltpu.VMEM((4, PIECE, 128), BF16),
    "ring": pltpu.VMEM((2, 4, PIECE, 128), BF16),
    "load_sem": pltpu.SemaphoreType.DMA((6, 2)),
    "shift_sem": pltpu.SemaphoreType.DMA((2, 2)),
    "pair_sem": pltpu.SemaphoreType.DMA((2, 2, 2, 4)),
    "fold_sem": pltpu.SemaphoreType.DMA((2, 3, 4)),
    "ring_sem": pltpu.SemaphoreType.DMA((2, 2, 4, 4)),
}
VMEM_MB = 44
LOADS = ("acts", "tops", "gains", "qkvs", "outs", "seeds")
AHEAD = ((0, 0), (1, 3), (0, 3))
BEHIND = ((0, 1), (1, 1), (0, 2))


def window(*refs):
    sources = refs[2:14]
    grads, grad_gain, grad_qkv, grad_out = refs[14:18]
    s = dict(zip(SCRATCH, refs[18:]))
    orders, offsets = s["orders"], s["offsets"]
    numbers = [
        pltpu.make_async_copy(refs[k], into, s["number_sem"].at[k]) for k, into in enumerate((orders, offsets))
    ]
    for copy in numbers:
        copy.start()

    section, replica = lax.axis_index("section"), lax.axis_index("dp")
    sections, replicas = lax.axis_size("section"), lax.axis_size("dp")
    low, core = section % 2, replica % 2
    height = (replica // 2) * 2 + low
    partner = (section, replica + 1 - 2 * core)
    across = (sections - 2 - section + 2 * low, replica)
    ways = (
        (section + 1 - 2 * low, (replica + 2 * low) % replicas),
        (section + 1 - 2 * low, (replica + replicas - 2 + 2 * low) % replicas),
    )
    nexts = (((section + 1) % sections, replica), ((section + sections - 1) % sections, replica))

    barrier = pltpu.get_barrier_semaphore()
    for peer in (partner, across, *ways, *nexts):
        pl.semaphore_signal(barrier, inc=1, device_id=peer, device_id_type=MESH)

    def load(name, c):
        where = LOADS.index(name)
        return pltpu.make_async_copy(sources[2 * where + c], s[name].at[pl.ds(c, 1)], s["load_sem"].at[where, c])

    def picked(c, slot):
        chosen = orders[1 - c, 0, slot]
        offset = jnp.where(chosen == 0, offsets[1 - c, 0, 0, 0], offsets[1 - c, 0, 0, 1])

        def rows_of(rows):
            return jnp.where(chosen == 0, s["acts"][c, 0, rows, :].astype(F32), s["acts"][c, 1, rows, :].astype(F32))

        return rows_of, offset

    def keep(c, slot):
        names = ("proj_t", "keys", "values", "soft", "soft_low")
        return (*(s[name].at[c] for name in names), s["att_t"].at[c, slot])

    def run_norm(c, slot):
        norm_rows(picked(c, slot)[0], s["gains"].at[c], s["normed"].at[c, slot], s["inverse"].at[c])

    def run_forward(c, slot):
        forward(picked(c, slot)[1], s["normed"].at[c, slot], s["qkvs"].at[c], keep(c, slot))

    def run_backward(c, slot, upstream, hooks=()):
        work = tuple(s[name] for name in ("att_grad", "score_grad", "grad", "normed_grad"))
        backward(
            picked(c, slot)[0], s["gains"].at[c], s["inverse"].at[c], s["qkvs"].at[c], s["outs"].at[c],
            upstream, keep(c, slot), work, s["grad_t"].at[c, slot], s["gain_sum"].at[c],
            grads.at[1 - c, 0, slot], hooks,
        )

    def remote(source, target, sems, device):
        return pltpu.make_async_remote_copy(
            src_ref=source, dst_ref=target, send_sem=sems[0], recv_sem=sems[1],
            device_id=device, device_id_type=MESH,
        )

    def shift(c):
        sems = (s["shift_sem"].at[0, c], s["shift_sem"].at[1, c])
        return remote(grads.at[1 - c, 0, 0], s["taken"].at[c], sems, nexts[c])

    def pair(c, b, j):
        sems = (s["pair_sem"].at[0, c, b, j], s["pair_sem"].at[1, c, b, j])
        rows = BLOCKS[b]
        return remote(s["pieces"].at[c, j, 1 - core, rows], s["paired"].at[c, j, rows], sems, partner)

    def fold(f, j):
        sems = (s["fold_sem"].at[0, f, j], s["fold_sem"].at[1, f, j])
        rows = FOLDS[f]
        return remote(s["own"].at[0, j, rows], s["mirror"].at[j, rows], sems, across)

    def add_pair(c, b, j):
        rows = BLOCKS[b]
        pair(c, b, j).wait_recv()
        total = s["pieces"][c, j, core, rows, :].astype(F32) + s["paired"][c, j, rows, :].astype(F32)
        s["own"][c, j, rows, :] = total.astype(BF16)

    def chip(c, j):
        return ((height + 3 + c + 2 * j) % replicas) // 2

    def take(c):
        load("seeds", c).wait()
        shift(c).wait_recv()

        @pl.when(section == (sections - 1) * c)
        def _():
            s["taken"][c] = s["seeds"][c]

    def make_out_terms(c):
        @pl.loop(0, 4)
        def _(j):
            att_t = [s["att_t"].at[c, k] for k in range(2)]
            out_terms(chip(c, j), att_t, [s["tops"].at[c], s["taken"].at[c]], s["pieces"].at[c, j])
            pair(c, 0, j).start()

    def make_qkv_terms(c):
        @pl.loop(0, 4)
        def _(j):
            grad_t, normed = ([s[name].at[c, k] for k in range(2)] for name in ("grad_t", "normed"))
            qkv_terms(chip(c, j), grad_t, normed, s["gain_sum"].at[c], s["pieces"].at[c, j])
            pair(c, 1, j).start()

    def send_out_folds():
        for j in (0, 1, 3, 2):
            add_pair(0, 0, j)
            fold(0, j).start()

    def send_qkv_folds():
        for first, second in ((0, 1), (3, 2)):
            for j in (first, second):
                add_pair(0, 1, j)
            for j, f in ((first, 2), (second, 1), (first, 1), (second, 2)):
                fold(f, j).start()

    def term(way, step):
        if step == 0:
            return s["own"].at[1, 0]
        mirrored, j = (AHEAD, BEHIND)[way][step - 1]
        return s["mirror"].at[j] if mirrored == 0 else s["own"].at[1, j]

    def hop(way, step, p):
        sems = (s["ring_sem"].at[0, way, step, p], s["ring_sem"].at[1, way, step, p])
        return remote(term(way, step).at[PARTS[p]], s["ring"].at[way, step, PARTS[p]], sems, ways[way])

    folded = set()

    def send_on(way, step, p):
        rows = PARTS[p]
        if step > 0:
            mirrored, j = (AHEAD, BEHIND)[way][step - 1]
            if mirrored == 0 and (FOLD_OF[p], j) not in folded:
                folded.add((FOLD_OF[p], j))
                fold(FOLD_OF[p], j).wait_recv()
            if step > 1 or p % 2 == way:
                hop(way, step - 1, p).wait_recv()
                mine = term(way, step)
                total = mine[rows, :].astype(F32) + s["ring"][way, step - 1, rows, :].astype(F32)
                mine[rows, :] = total.astype(BF16)
        hop(way, step, p).start()

    def ring_step(b, step):
        if step == 0:
            for way in range(2):
                send_on(way, 0, 2 * b + way)
            return
        for turn in range(2):
            for way in range(2):
                send_on(way, step, 2 * b + (1 - way if turn == 0 else way))

    def final(b):
        for way in range(2):
            for p in (2 * b, 2 * b + 1):
                hop(way, 3, p).wait_recv()
        rows = BLOCKS[b]
        return s["own"][1, 2, rows].astype(F32) + s["ring"][0, 3, rows].astype(F32) + s["ring"][1, 3, rows].astype(F32)

    def ring_out_start():
        for j in (0, 3, 1, 2):
            add_pair(1, 0, j)
        ring_step(0, 0)

    for c in range(2):
        for name in ("acts", "gains", "qkvs", "outs", "tops"):
            load(name, c).start()
    for c in range(2):
        load("seeds", c).start()
    s["gain_sum"][...] = jnp.zeros_like(s["gain_sum"])

    for copy in numbers:
        copy.wait()
    for c in range(2):
        load("acts", c).wait()
        load("gains", c).wait()
        run_norm(c, 0)
        load("qkvs", c).wait()
        run_forward(c, 0)
        load("outs", c).wait()
        load("tops", c).wait()
        run_backward(c, 0, s["tops"].at[c])
        if c == 0:
            pl.semaphore_wait(barrier, 6)
        shift(c).start()
    for c in range(2):
        run_norm(c, 1)
        run_forward(c, 1)

    take(0)
    make_out_terms(0)
    run_backward(0, 1, s["taken"].at[0], {0: send_out_folds})
    make_qkv_terms(0)
    take(1)
    make_out_terms(1)
    run_backward(1, 1, s["taken"].at[1], {"start": send_qkv_folds, 0: ring_out_start})
    ring_step(0, 1)
    make_qkv_terms(1)
    ring_step(0, 2)
    for j in (0, 3, 1, 2):
        add_pair(1, 1, j)
    ring_step(1, 0)
    ring_step(0, 3)
    for step in range(1, 4):
        ring_step(1, step)

    total = final(0)
    for k in range(8):
        grad_out[0, :, k * 128 : k * 128 + 128] = total[k * HD : k * HD + HD, :]
    total = final(1)
    for n in range(3):
        grad_qkv[0, :, n * 256 : n * 256 + 256] = total[n * 256 : n * 256 + 256, :].T
    grad_gain[...] = total[QKV : QKV + 1, :]

    for c in range(2):
        shift(c).wait_send()
        for b in range(2):
            for j in range(4):
                pair(c, b, j).wait_send()
    for j in range(4):
        for f in range(3):
            fold(f, j).wait_send()
    for way in range(2):
        for step in range(4):
            for p in range(4):
                if step > 0 or p % 2 == way:
                    hop(way, step, p).wait_send()


def shards(
    act_down, act_up, grad_down, grad_up, seed_down, seed_up, gain_down, qkv_down, outproj_down,
    gain_up, qkv_up, outproj_up, doc_offsets, slot_order,
):
    shapes = (
        jax.ShapeDtypeStruct((2, 1, 2, SEQ, D), BF16),
        jax.ShapeDtypeStruct((1, 128), F32),
        jax.ShapeDtypeStruct((1, 128, QKV), F32),
        jax.ShapeDtypeStruct((1, HD, D), F32),
    )
    whole = pl.BlockSpec(memory_space=pltpu.VMEM)
    outside = pl.BlockSpec(memory_space=pltpu.HBM)
    return pl.pallas_call(
        window,
        in_specs=[outside] * 14,
        out_specs=[whole] * 4,
        out_shape=shapes,
        scratch_shapes=list(SCRATCH.values()),
        compiler_params=pltpu.CompilerParams(
            vmem_limit_bytes=VMEM_MB * 2**20, collective_id=0, has_side_effects=True
        ),
    )(
        *(
            pltpu.with_memory_space_constraint(x, pltpu.HBM)
            for x in (
                slot_order, doc_offsets.transpose(0, 1, 3, 2), act_up, act_down, grad_up, grad_down, gain_up[None], gain_down[None],
                qkv_up, qkv_down, outproj_up, outproj_down, seed_up[None], seed_down[None],
            )
        ),
    )


def solution(mesh):
    return jax.shard_map(
        shards,
        mesh=mesh,
        in_specs=(
            P("section", None, "dp", None),
            P("section", None, "dp", None),
            P("section", "dp", None),
            P("section", "dp", None),
            P("dp", None),
            P("dp", None),
            P("section", None),
            P("section", None, None),
            P("section", None, None),
            P("section", None),
            P("section", None, None),
            P("section", None, None),
            P(None, "section", None, "dp"),
            P(None, "section", None),
        ),
        out_specs=(
            P(None, "section", None, "dp", None),
            P("section", "dp"),
            P("section", "dp", None),
            P("section", "dp", None),
        ),
        check_vma=False,
    )
```

time: 90.2 us -> 78.1 us (0.87); the launches traced: 88.6 us -> 78 us
  Pallas kernels: 78.4 us -> 74.1 us
  local copies, waits for them, and re-layouts: 6.81 us -> 3.28 us
  other arithmetic: 2.68 us -> 0 us
    pallas_call x1, Pallas kernels: 78.4 us -> 74.1 us  [shards(): pl.pallas_call(window, in_specs=[outside] * 14, out_specs=[whole] * 4, ou...]
    unnamed x2 -> x0, other arithmetic: 2.68 us -> none
    unnamed x11 -> x4, local copies, waits for them, and re-layouts: 5.63 us -> 3.28 us
    reshape x2 -> x0, local copies, waits for them, and re-layouts: 1.19 us -> none  [the longest x1 0.59 us: shards(): doc_offsets.reshape(4)]
where the time goes in v2:
time: 78.1 us; the launch traced here: 78 us
  Pallas kernels  74.1 us (95%)
  local copies, waits for them, and re-layouts  3.28 us (4%)
    pallas_call x1, Pallas kernels, shards(): pl.pallas_call(window, in_specs=[outside] * 14, out_specs=[whole] * 4, ou...  74.1 us
    unnamed x4, local copies, waits for them, and re-layouts  3.28 us

profile of v2, /device:TPU:66, one launch (start us, length us, event | category | flops | bytes accessed | tf_op | source)
XLA Modules:
  0.0 78.0 jit_solution(6091332543407463364)
XLA Ops:
  0.6 74.1 %shard_map.165 = (bf16[2,1,2,256,1024]{4,3,2,1,0:T(8,128)(2,1)S(1)}, f32[1,128]{1,0:T(1,128)S(1)}, f32[1,128,768]{2,1,0:T(8,128)S(1)}, f32[1,64,1024]{2,1,0:T(8,128)S(1)}) custom-call(s32[2,1,2]{2,1,0:T(1,128)} %refs_0_.1, s32[2,1,1,2]{3,2,1,0:T(1,128)} %bitcast.11, bf16[1,2,256,1024]{3,2,1,0:T(8,128)(2,1)} %refs_2_.1, bf16[1,2,256,1024]{3,2,1,0:T(8,128)(2,1)} %refs_3_.1, ...), custom_call_target="tpu_custom_call" | custom-call | tf_op jit(solution)/shard_map/pallas_call | solution.py:435
  74.7 1.3 %copy.23 = bf16[2,1,2,256,1024]{4,3,2,1,0:T(8,128)(2,1)} copy(bf16[2,1,2,256,1024]{4,3,2,1,0:T(8,128)(2,1)S(1)} %get-tuple-element.8) | data formatting | bytes 4194304
  76.1 0.5 copy.24
  76.6 0.7 copy.25
  77.3 0.7 copy.26

commit v3 on v2

--- a/solution.py
+++ b/solution.py
@@ -1,4 +1,4 @@
-import functools
+import math
 
 import jax
 import jax.numpy as jnp
@@ -18,6 +18,8 @@
 PARTS = (slice(0, 256), slice(256, QW), slice(QW, 896), slice(896, PIECE))
 FOLD_OF = (0, 0, 1, 2)
 MESH = pl.DeviceIdType.MESH
+SCALE = HD**-0.5
+SCALE_2 = SCALE * math.log2(math.e)
 
 
 def nn(a, b):
@@ -26,6 +28,13 @@
 
 def nt(a, b):
     return lax.dot_general(a, b, (((1,), (1,)), ((), ())), preferred_element_type=F32)
+
+
+def stagger(stages):
+    for step in range(HEADS + len(stages) - 1):
+        for k, stage in enumerate(stages):
+            if 0 <= step - k < HEADS:
+                stage(step - k)
 
 
 def norm_rows(x, gain, normed, inverse):
@@ -37,7 +46,15 @@
         inverse[rows, :] = jnp.broadcast_to(inv, (ROWS, 128))
 
 
-def forward(offset, normed, qkv, keep):
+def set_ceiling(offset, ceiling):
+    for half, depth in ((0, 128), (1, 256)):
+        at_key = lax.broadcasted_iota(jnp.int32, (depth, 128), 0)
+        at_query = lax.broadcasted_iota(jnp.int32, (depth, 128), 1) + half * 128
+        allowed = (at_key <= at_query) & ((at_query < offset) | (at_key >= offset))
+        ceiling[:depth, half * 128 : half * 128 + 128] = jnp.where(allowed, jnp.inf, -1e30)
+
+
+def forward(ceiling, normed, qkv, keep):
     proj_t, keys, values, soft, soft_low, att_t = keep
     for n in range(3):
         cols = slice(n * 256, n * 256 + 256)
@@ -47,57 +64,67 @@
             low = part.astype(BF16)
             keys[0], keys[1] = low[:, :64], low[:, 64:128]
             values[0], values[1] = low[:, 128:192], low[:, 192:256]
-    for head in range(HEADS):
-        group = head // GROUP
+    def score(head):
         rows = slice(head * HD, head * HD + HD)
-        scores = nn(keys[group], proj_t[rows, :])
+        soft[head] = nn(keys[head // GROUP], proj_t[rows, :])
+
+    def normalize(head):
         for half, depth in ((0, 128), (1, 256)):
             cols = slice(half * 128, half * 128 + 128)
-            at_key = lax.broadcasted_iota(jnp.int32, (depth, 128), 0)
-            at_query = lax.broadcasted_iota(jnp.int32, (depth, 128), 1) + half * 128
-            allowed = (at_key <= at_query) & ((at_query < offset) | (at_key >= offset))
-            part = jnp.where(allowed, scores[:depth, cols] * (HD**-0.5), -1e30)
-            raised = jnp.exp(part - jnp.max(part, axis=0, keepdims=True))
+            part = jnp.minimum(soft[head, :depth, cols] * SCALE_2, ceiling[:depth, cols])
+            raised = jnp.exp2(part - jnp.max(part, axis=0, keepdims=True))
             weights = raised * (1.0 / jnp.sum(raised, axis=0, keepdims=True))
             soft[head, :depth, cols] = weights
             soft_low[head, :depth, cols] = weights.astype(BF16)
         soft_low[head, 128:, :128] = jnp.zeros((128, 128), BF16)
-        value_rows = slice(QW + 128 + group * HD, QW + 128 + group * HD + HD)
+
+    def attend(head):
+        rows = slice(head * HD, head * HD + HD)
+        value_rows = slice(QW + 128 + head // GROUP * HD, QW + 128 + head // GROUP * HD + HD)
         att_t[rows, :] = nn(proj_t[value_rows, :], soft_low[head]).astype(BF16)
+
+    stagger((score, normalize, attend))
 
 
 def backward(x, gain, inverse, qkv, outproj, upstream, keep, work, grad_t, gain_sum, result, hooks=()):
     hooks = dict(hooks)
     proj_t, keys, values, soft, soft_low, _ = keep
-    att_grad, score_grad, grad, normed_grad = work
+    att_grad, soft_grad, score_grad, grad, normed_grad = work
     for m in range(2):
         rows = slice(m * 256, m * 256 + 256)
         att_grad[rows, :] = nt(outproj[rows, :], upstream[...]).astype(BF16)
     if "start" in hooks:
         hooks["start"]()
-    for group in range(HEADS // GROUP):
-        key_sum = jnp.zeros((HD, SEQ), F32)
-        value_sum = jnp.zeros((HD, SEQ), F32)
+    sums = [[None, None], [None, None]]
+
+    def soften(head):
+        rows = slice(head * HD, head * HD + HD)
+        soft_grad[head % 4] = nn(values[head // GROUP], att_grad[rows, :])
+
+    def combine(head):
+        for half, depth in ((0, 128), (1, 256)):
+            cols = slice(half * 128, half * 128 + 128)
+            weights = soft[head, :depth, cols]
+            part = soft_grad[head % 4, :depth, cols]
+            total = jnp.sum(weights * part, axis=0, keepdims=True)
+            score_grad[head, :depth, cols] = (weights * (part - total)).astype(BF16)
+        score_grad[head, 128:, :128] = jnp.zeros((128, 128), BF16)
+
+    def project(head):
+        group = head // GROUP
+        rows = slice(head * HD, head * HD + HD)
         key_rows = slice(QW + group * HD, QW + group * HD + HD)
         value_rows = slice(QW + 128 + group * HD, QW + 128 + group * HD + HD)
-        for head in range(group * GROUP, group * GROUP + GROUP):
-            rows = slice(head * HD, head * HD + HD)
-            low = att_grad[rows, :]
-            soft_grad = nn(values[group], low)
-            for half, depth in ((0, 128), (1, 256)):
-                cols = slice(half * 128, half * 128 + 128)
-                weights = soft[head, :depth, cols]
-                part = soft_grad[:depth, cols]
-                total = jnp.sum(weights * part, axis=0, keepdims=True)
-                score_grad[head, :depth, cols] = (weights * (part - total) * (HD**-0.5)).astype(BF16)
-            score_grad[head, 128:, :128] = jnp.zeros((128, 128), BF16)
-            grad_t[rows, :] = nn(proj_t[key_rows, :], score_grad[head]).astype(BF16)
-            key_sum = key_sum + nt(proj_t[rows, :], score_grad[head])
-            value_sum = value_sum + nt(low, soft_low[head])
-        grad_t[key_rows, :] = key_sum.astype(BF16)
-        grad_t[value_rows, :] = value_sum.astype(BF16)
-        if group in hooks:
-            hooks[group]()
+        grad_t[rows, :] = (nn(proj_t[key_rows, :], score_grad[head]) * SCALE).astype(BF16)
+        for k, part in enumerate((nt(proj_t[rows, :], score_grad[head]), nt(att_grad[rows, :], soft_low[head]))):
+            sums[group][k] = part if sums[group][k] is None else sums[group][k] + part
+        if head % GROUP == GROUP - 1:
+            grad_t[key_rows, :] = (sums[group][0] * SCALE).astype(BF16)
+            grad_t[value_rows, :] = sums[group][1].astype(BF16)
+            if group in hooks:
+                hooks[group]()
+
+    stagger((soften, combine, project))
     for n in range(3):
         cols = slice(n * 256, n * 256 + 256)
         grad[:, cols] = grad_t[cols, :].T
@@ -166,7 +193,9 @@
     "values": pltpu.VMEM((2, 2, SEQ, HD), BF16),
     "soft": pltpu.VMEM((2, HEADS, SEQ, SEQ), F32),
     "soft_low": pltpu.VMEM((2, HEADS, SEQ, SEQ), BF16),
+    "ceiling": pltpu.VMEM((SEQ, SEQ), F32),
     "att_grad": pltpu.VMEM((QW, SEQ), BF16),
+    "soft_grad": pltpu.VMEM((4, SEQ, SEQ), F32),
     "score_grad": pltpu.VMEM((HEADS, SEQ, SEQ), BF16),
     "grad": pltpu.VMEM((SEQ, QKV), BF16),
     "normed_grad": pltpu.VMEM((SEQ, D), F32),
@@ -235,10 +264,11 @@
         norm_rows(picked(c, slot)[0], s["gains"].at[c], s["normed"].at[c, slot], s["inverse"].at[c])
 
     def run_forward(c, slot):
-        forward(picked(c, slot)[1], s["normed"].at[c, slot], s["qkvs"].at[c], keep(c, slot))
+        set_ceiling(picked(c, slot)[1], s["ceiling"])
+        forward(s["ceiling"], s["normed"].at[c, slot], s["qkvs"].at[c], keep(c, slot))
 
     def run_backward(c, slot, upstream, hooks=()):
-        work = tuple(s[name] for name in ("att_grad", "score_grad", "grad", "normed_grad"))
+        work = tuple(s[name] for name in ("att_grad", "soft_grad", "score_grad", "grad", "normed_grad"))
         backward(
             picked(c, slot)[0], s["gains"].at[c], s["inverse"].at[c], s["qkvs"].at[c], s["outs"].at[c],
             upstream, keep(c, slot), work, s["grad_t"].at[c, slot], s["gain_sum"].at[c],
@@ -283,15 +313,13 @@
             s["taken"][c] = s["seeds"][c]
 
     def make_out_terms(c):
-        @pl.loop(0, 4)
-        def _(j):
+        for j in range(4):
             att_t = [s["att_t"].at[c, k] for k in range(2)]
             out_terms(chip(c, j), att_t, [s["tops"].at[c], s["taken"].at[c]], s["pieces"].at[c, j])
             pair(c, 0, j).start()
 
     def make_qkv_terms(c):
-        @pl.loop(0, 4)
-        def _(j):
+        for j in range(4):
             grad_t, normed = ([s[name].at[c, k] for k in range(2)] for name in ("grad_t", "normed"))
             qkv_terms(chip(c, j), grad_t, normed, s["gain_sum"].at[c], s["pieces"].at[c, j])
             pair(c, 1, j).start()

time: 78.1 us -> 75.4 us (0.965)
  Pallas kernels: 74.1 us -> 71.4 us
    pallas_call x1, Pallas kernels: 74.1 us -> 71.4 us  [shards(): pl.pallas_call(window, in_specs=[outside] * 14, out_specs=[whole] * 4, ou...]
where the time goes in v3:
time: 75.4 us; the launch traced here: 75.3 us
  Pallas kernels  71.4 us (95%)
  local copies, waits for them, and re-layouts  3.28 us (4%)
    pallas_call x1, Pallas kernels, shards(): pl.pallas_call(window, in_specs=[outside] * 14, out_specs=[whole] * 4, ou...  71.4 us
    unnamed x4, local copies, waits for them, and re-layouts  3.28 us

profile of v3, /device:TPU:66, one launch (start us, length us, event | category | flops | bytes accessed | tf_op | source)
XLA Modules:
  0.0 75.3 jit_solution(6750983418843274842)
XLA Ops:
  0.6 71.4 %shard_map.165 = (bf16[2,1,2,256,1024]{4,3,2,1,0:T(8,128)(2,1)S(1)}, f32[1,128]{1,0:T(1,128)S(1)}, f32[1,128,768]{2,1,0:T(8,128)S(1)}, f32[1,64,1024]{2,1,0:T(8,128)S(1)}) custom-call(s32[2,1,2]{2,1,0:T(1,128)} %refs_0_.1, s32[2,1,1,2]{3,2,1,0:T(1,128)} %bitcast.11, bf16[1,2,256,1024]{3,2,1,0:T(8,128)(2,1)} %refs_2_.1, bf16[1,2,256,1024]{3,2,1,0:T(8,128)(2,1)} %refs_3_.1, ...), custom_call_target="tpu_custom_call" | custom-call | tf_op jit(solution)/shard_map/pallas_call | solution.py:463
  72.0 1.3 %copy.23 = bf16[2,1,2,256,1024]{4,3,2,1,0:T(8,128)(2,1)} copy(bf16[2,1,2,256,1024]{4,3,2,1,0:T(8,128)(2,1)S(1)} %get-tuple-element.8) | data formatting | bytes 4194304
  73.4 0.5 copy.24
  73.9 0.7 copy.25
  74.6 0.7 copy.26

commit v4 on v3

--- a/solution.py
+++ b/solution.py
@@ -54,7 +54,7 @@
         ceiling[:depth, half * 128 : half * 128 + 128] = jnp.where(allowed, jnp.inf, -1e30)
 
 
-def forward(ceiling, normed, qkv, keep):
+def forward(ceiling, normed, qkv, keep, late=False):
     proj_t, keys, values, soft, soft_low, att_t = keep
     for n in range(3):
         cols = slice(n * 256, n * 256 + 256)
@@ -83,6 +83,9 @@
         value_rows = slice(QW + 128 + head // GROUP * HD, QW + 128 + head // GROUP * HD + HD)
         att_t[rows, :] = nn(proj_t[value_rows, :], soft_low[head]).astype(BF16)
 
+    if late:
+        stagger((score, normalize))
+        return attend
     stagger((score, normalize, attend))
 
 
@@ -128,10 +131,14 @@
     for n in range(3):
         cols = slice(n * 256, n * 256 + 256)
         grad[:, cols] = grad_t[cols, :].T
-    for n in range(4):
-        cols = slice(n * 256, n * 256 + 256)
-        normed_grad[:, cols] = nt(grad[...], qkv[cols, :])
     for step in range(SEQ // ROWS):
+        if step % 4 == 0:
+            half = slice(step * ROWS, step * ROWS + 128)
+            for n in range(4):
+                cols = slice(n * 256, n * 256 + 256)
+                normed_grad[half, cols] = nt(grad[half, :], qkv[cols, :])
+            if step == 4 and "half" in hooks:
+                hooks["half"]()
         rows = slice(step * ROWS, step * ROWS + ROWS)
         inv = inverse[rows, :][:, :1]
         scaled = x(rows) * inv
@@ -205,7 +212,7 @@
     "mirror": pltpu.VMEM((4, PIECE, 128), BF16),
     "ring": pltpu.VMEM((2, 4, PIECE, 128), BF16),
     "load_sem": pltpu.SemaphoreType.DMA((6, 2)),
-    "shift_sem": pltpu.SemaphoreType.DMA((2, 2)),
+    "shift_sem": pltpu.SemaphoreType.DMA((2, 2, 2)),
     "pair_sem": pltpu.SemaphoreType.DMA((2, 2, 2, 4)),
     "fold_sem": pltpu.SemaphoreType.DMA((2, 3, 4)),
     "ring_sem": pltpu.SemaphoreType.DMA((2, 2, 4, 4)),
@@ -263,9 +270,9 @@
     def run_norm(c, slot):
         norm_rows(picked(c, slot)[0], s["gains"].at[c], s["normed"].at[c, slot], s["inverse"].at[c])
 
-    def run_forward(c, slot):
+    def run_forward(c, slot, late=False):
         set_ceiling(picked(c, slot)[1], s["ceiling"])
-        forward(s["ceiling"], s["normed"].at[c, slot], s["qkvs"].at[c], keep(c, slot))
+        return forward(s["ceiling"], s["normed"].at[c, slot], s["qkvs"].at[c], keep(c, slot), late)
 
     def run_backward(c, slot, upstream, hooks=()):
         work = tuple(s[name] for name in ("att_grad", "soft_grad", "score_grad", "grad", "normed_grad"))
@@ -281,9 +288,10 @@
             device_id=device, device_id_type=MESH,
         )
 
-    def shift(c):
-        sems = (s["shift_sem"].at[0, c], s["shift_sem"].at[1, c])
-        return remote(grads.at[1 - c, 0, 0], s["taken"].at[c], sems, nexts[c])
+    def shift(c, h):
+        sems = (s["shift_sem"].at[0, c, h], s["shift_sem"].at[1, c, h])
+        rows = pl.ds(h * 128, 128)
+        return remote(grads.at[1 - c, 0, 0, rows], s["taken"].at[c, rows], sems, nexts[c])
 
     def pair(c, b, j):
         sems = (s["pair_sem"].at[0, c, b, j], s["pair_sem"].at[1, c, b, j])
@@ -306,7 +314,8 @@
 
     def take(c):
         load("seeds", c).wait()
-        shift(c).wait_recv()
+        for h in range(2):
+            shift(c, h).wait_recv()
 
         @pl.when(section == (sections - 1) * c)
         def _():
@@ -379,9 +388,16 @@
         return s["own"][1, 2, rows].astype(F32) + s["ring"][0, 3, rows].astype(F32) + s["ring"][1, 3, rows].astype(F32)
 
     def ring_out_start():
-        for j in (0, 3, 1, 2):
+        add_pair(1, 0, 0)
+        ring_step(0, 0)
+
+    def start_both():
+        ring_out_start()
+        send_qkv_folds()
+
+    def add_out_pairs():
+        for j in (3, 1, 2):
             add_pair(1, 0, j)
-        ring_step(0, 0)
 
     for c in range(2):
         for name in ("acts", "gains", "qkvs", "outs", "tops"):
@@ -397,31 +413,39 @@
         load("gains", c).wait()
         run_norm(c, 0)
         load("qkvs", c).wait()
-        run_forward(c, 0)
+        attend = run_forward(c, 0, late=True)
         load("outs", c).wait()
         load("tops", c).wait()
-        run_backward(c, 0, s["tops"].at[c])
         if c == 0:
             pl.semaphore_wait(barrier, 6)
-        shift(c).start()
+            run_backward(c, 0, s["tops"].at[c], {"half": shift(c, 0).start})
+            shift(c, 1).start()
+        else:
+            run_backward(c, 0, s["tops"].at[c])
+        for head in range(HEADS):
+            attend(head)
     for c in range(2):
         run_norm(c, 1)
         run_forward(c, 1)
 
+    for h in range(2):
+        shift(0, h).wait_send()
+        shift(1, h).start()
     take(0)
     make_out_terms(0)
     run_backward(0, 1, s["taken"].at[0], {0: send_out_folds})
     make_qkv_terms(0)
     take(1)
     make_out_terms(1)
-    run_backward(1, 1, s["taken"].at[1], {"start": send_qkv_folds, 0: ring_out_start})
+    run_backward(1, 1, s["taken"].at[1], {"start": start_both, 0: add_out_pairs})
     ring_step(0, 1)
     make_qkv_terms(1)
     ring_step(0, 2)
-    for j in (0, 3, 1, 2):
-        add_pair(1, 1, j)
+    add_pair(1, 1, 0)
     ring_step(1, 0)
     ring_step(0, 3)
+    for j in (3, 1, 2):
+        add_pair(1, 1, j)
     for step in range(1, 4):
         ring_step(1, step)
 
@@ -434,7 +458,9 @@
     grad_gain[...] = total[QKV : QKV + 1, :]
 
     for c in range(2):
-        shift(c).wait_send()
+        if c == 1:
+            for h in range(2):
+                shift(c, h).wait_send()
         for b in range(2):
             for j in range(4):
                 pair(c, b, j).wait_send()

time: 75.4 us -> 75.2 us (level)
  no operation moved by 1% of the time
where the time goes in v4:
time: 75.2 us; the launch traced here: 75.1 us
  Pallas kernels  71.2 us (95%)
  local copies, waits for them, and re-layouts  3.28 us (4%)
    pallas_call x1, Pallas kernels, shards(): pl.pallas_call(window, in_specs=[outside] * 14, out_specs=[whole] * 4, ou...  71.2 us
    unnamed x4, local copies, waits for them, and re-layouts  3.28 us

profile of v4, /device:TPU:66, one launch (start us, length us, event | category | flops | bytes accessed | tf_op | source)
XLA Modules:
  0.0 75.1 jit_solution(1479476949370025985)
XLA Ops:
  0.6 71.2 %shard_map.165 = (bf16[2,1,2,256,1024]{4,3,2,1,0:T(8,128)(2,1)S(1)}, f32[1,128]{1,0:T(1,128)S(1)}, f32[1,128,768]{2,1,0:T(8,128)S(1)}, f32[1,64,1024]{2,1,0:T(8,128)S(1)}) custom-call(s32[2,1,2]{2,1,0:T(1,128)} %refs_0_.1, s32[2,1,1,2]{3,2,1,0:T(1,128)} %bitcast.11, bf16[1,2,256,1024]{3,2,1,0:T(8,128)(2,1)} %refs_2_.1, bf16[1,2,256,1024]{3,2,1,0:T(8,128)(2,1)} %refs_3_.1, ...), custom_call_target="tpu_custom_call" | custom-call | tf_op jit(solution)/shard_map/pallas_call | solution.py:489
  71.8 1.3 %copy.23 = bf16[2,1,2,256,1024]{4,3,2,1,0:T(8,128)(2,1)} copy(bf16[2,1,2,256,1024]{4,3,2,1,0:T(8,128)(2,1)S(1)} %get-tuple-element.8) | data formatting | bytes 4194304
  73.2 0.5 copy.24
  73.7 0.7 copy.25
  74.4 0.7 copy.26
